TPU v7x, 32 devices: a whole 2x2x4 slice. The times are simulated.
32 devices in a mesh: comp: 2 (over x), gy: 4 (over y, core), gx: 4 (over z).
Axes of the slice: x: 2, y: 2, z: 4, core: 2. Of those that a mesh axis runs over, the one named last changes fastest.
Arguments:
- state: float32 [2, 8, 512, 512], P('comp', None, 'gy', 'gx'), may hold values from -6 to 6
- target: float32 [2, 8, 512, 512], P('comp', None, 'gy', 'gx'), may hold values from -2.5 to 0.5
- land_mask: int32 [2, 512, 512], P('comp', 'gy', 'gx'), may hold values 0 or 1
- diffusivity: float32 [2, 8], replicated, may hold values from 0.03 to 0.24
- coupling: float32 [2, 8, 4], replicated, may hold values from -3 to 3
- w_in: bfloat16 [16, 256], replicated, may hold values from -1.5 to 1.5
- b_in: float32 [256], replicated, may hold values from -3 to 3
- w_mid: bfloat16 [256, 256], replicated, may hold values from -0.375 to 0.375
- b_mid: float32 [256], replicated, may hold values from -3 to 3
- w_out: bfloat16 [256, 4], replicated, may hold values from -0.375 to 0.375
- b_out: float32 [4], replicated, may hold values from -3 to 3
- remap_weight: bfloat16 [2, 4, 4, 16, 4, 128, 128], P('comp', 'gy', 'gx'), may hold values from -0.5 to 0.5
- remap_source: int32 [2, 4, 4, 16, 4], P('comp', 'gy', 'gx'), may hold values from 0 to 127
- remap_target: int32 [2, 4, 4, 16, 4], P('comp', 'gy', 'gx'), may hold values from 0 to 127
- remap_count: int32 [2, 4, 4, 16], P('comp', 'gy', 'gx'), may hold values from 0 to 4, as said below
Outputs:
- new_state: float32 [2, 8, 512, 512], P('comp', None, 'gy', 'gx')
- state_adjoint: float32 [2, 8, 512, 512], P('comp', None, 'gy', 'gx')
- grad_w_in: float32 [16, 256], replicated
- grad_b_in: float32 [256], replicated
- grad_w_mid: float32 [256, 256], replicated
- grad_b_mid: float32 [256], replicated
- grad_w_out: float32 [256, 4], replicated
- grad_b_out: float32 [4], replicated
Inputs may be any that keep to these rules, and one draw needn't show every extreme that they name: remap_count[c, i, j, q] leading slots of the pair are in use, the rest are padding. A pair has slots in use exactly where receiving tile q lies within 2 tile rows of i and in a tile column within 2 of j (periodic), or, for a sender in the top tile row, where q lies in the top tile row within 1 column (periodic) of column 3 - j; such pairs use 1 slot or more; for each component one receiving tile has all 4 slots in use from every such sending tile.
All inputs are finite; a program needn't handle non-finite values. No bound on the sum of `land_mask` on one device may be relied on, other than what follows from the above.
Results may differ from a plain program's by a relative error of at most 0.0037.
Values may be sent and summed in bfloat16 or wider, within the bound.
No kernel may reach another device: no remote copies, remote signals or barrier semaphores. Data moves between devices by JAX's collectives and lax.ppermute only.
A program may use at most 64 MiB of HBM per device.

v0:
```python
import math
import jax
import jax.numpy as jnp
from jax import lax
from jax.sharding import PartitionSpec as P

PRECISE = lax.Precision.HIGHEST


def extended(cells, sides, width, closed):
    for axis, dim in sides:
        count = lax.axis_size(axis)
        ends = count if closed else count - 1
        head = lax.slice_in_dim(cells, 0, width, axis=dim)
        tail = lax.slice_in_dim(cells, cells.shape[dim] - width, cells.shape[dim], axis=dim)
        cells = jnp.concatenate(
            [
                lax.ppermute(tail, axis, [(i, (i + 1) % count) for i in range(ends)]),
                cells,
                lax.ppermute(head, axis, [((i + 1) % count, i) for i in range(ends)]),
            ],
            axis=dim,
        )
    return cells


def partner(block, axis, stride):
    count = lax.axis_size(axis)
    route = []
    for low in range(count):
        high = low | 1 << stride
        if high != low and high < count:
            route += [(low, high), (high, low)]
    return lax.ppermute(block, axis, route)


def silu_slope(preact):
    sigmoid_value = jax.nn.sigmoid(preact)
    return sigmoid_value * (1.0 + preact * (1.0 - sigmoid_value))


def laplace(surface, on_fold):
    wide_field = extended(surface, (("gx", 2),), 1, True)
    tall_field = extended(surface, (("gy", 1),), 1, False)
    top_row = surface[:, -1, :]
    mirrored = top_row[:, ::-1]
    for bit_index in range(lax.axis_size("gx").bit_length() - 1):
        mirrored = partner(mirrored, "gx", bit_index)
    north_rows = tall_field[:, 2:, :]
    north_rows = north_rows.at[:, -1, :].add(jnp.where(on_fold, mirrored, 0.0))
    return (
        wide_field[:, :, 2:]
        + wide_field[:, :, :-2]
        + tall_field[:, :-2, :]
        + north_rows
        - 4.0 * surface
    )


def forward_route(outgoing):
    relayed = lax.all_to_all(outgoing, ("gy", "gx"), split_axis=0, concat_axis=0, tiled=True)
    arrived = partner(relayed, "comp", 0)
    return arrived


def return_route(outgoing):
    relayed = lax.all_to_all(outgoing, ("gy", "gx"), split_axis=0, concat_axis=0, tiled=True)
    arrived = partner(relayed, "comp", 0)
    return arrived


def shards(
    state,
    target,
    land_mask,
    diffusivity,
    coupling,
    w_in,
    b_in,
    w_mid,
    b_mid,
    w_out,
    b_out,
    remap_weight,
    remap_source,
    remap_target,
    remap_count,
):
    comp_index = lax.axis_index("comp")
    is_ocean = comp_index == 1
    on_fold = jnp.logical_and(is_ocean, lax.axis_index("gy") == lax.axis_size("gy") - 1)
    surface = state[0]
    channels, tile_rows, tile_width = surface.shape
    cell_count = tile_rows * tile_width
    peer_count = remap_source.shape[3]
    slot_count = remap_source.shape[4]
    pair_count = peer_count * slot_count
    wet_mask = land_mask[0].astype(jnp.float32).reshape(1, cell_count)
    diff_mask = jnp.where(is_ocean, wet_mask, 1.0)
    diffuse_rate = diffusivity[comp_index]
    couple = coupling[comp_index]
    rounded = surface.astype(jnp.bfloat16)
    source = remap_source[0, 0, 0].reshape(pair_count)
    kernels = remap_weight[0, 0, 0].reshape(pair_count, tile_width, tile_width)
    slot_index = lax.broadcasted_iota(jnp.int32, (peer_count, slot_count), 1)
    live_mask = (
        (slot_index < remap_count[0, 0, 0][:, None]).astype(jnp.float32).reshape(pair_count, 1, 1)
    )
    picked = rounded[:, source, :]
    outgoing = (
        jnp.einsum("cki,kij->kcj", picked, kernels, preferred_element_type=jnp.float32) * live_mask
    )
    arrived = forward_route(outgoing.reshape(peer_count, slot_count, channels, tile_width))
    laplacian = laplace(surface, on_fold).reshape(channels, cell_count)
    row_index = lax.broadcasted_iota(jnp.int32, (tile_rows, pair_count), 0)
    landing = (row_index == remap_target[0, 0, 0].reshape(1, pair_count)).astype(jnp.float32)
    remapped = jnp.einsum(
        "tk,kcj->ctj", landing, arrived.reshape(pair_count, channels, tile_width), precision=PRECISE
    )
    own_fields = rounded.reshape(channels, cell_count)
    other_fields = remapped.astype(jnp.bfloat16).reshape(channels, cell_count)
    features = jnp.concatenate(
        [
            jnp.where(is_ocean, other_fields, own_fields),
            jnp.where(is_ocean, own_fields, other_fields),
        ],
        axis=0,
    )
    current = surface.reshape(channels, cell_count)
    goal = target[0].reshape(channels, cell_count)
    block_size = math.gcd(cell_count, 2048)

    def advance(block_index, loop_state):
        new_fields, misfits, feature_cots, gradients = loop_state
        offset = block_index * block_size

        def take_block(array):
            return lax.dynamic_slice_in_dim(array, offset, block_size, 1)

        feature_block = take_block(features)
        wet_block = take_block(wet_mask)
        diff_block = take_block(diff_mask)
        pre_first = (
            jnp.einsum("fh,fn->hn", w_in, feature_block, preferred_element_type=jnp.float32)
            + b_in[:, None]
        )
        hidden_first = jax.nn.silu(pre_first).astype(jnp.bfloat16)
        pre_second = (
            jnp.einsum("hk,hn->kn", w_mid, hidden_first, preferred_element_type=jnp.float32)
            + b_mid[:, None]
        )
        hidden_second = jax.nn.silu(pre_second).astype(jnp.bfloat16)
        fluxes = (
            jnp.einsum("ho,hn->on", w_out, hidden_second, preferred_element_type=jnp.float32)
            + b_out[:, None]
        ) * wet_block
        updated = (
            take_block(current)
            + diffuse_rate[:, None] * diff_block * take_block(laplacian)
            + jnp.dot(couple, fluxes, precision=PRECISE)
        )
        misfit = updated - take_block(goal)
        flux_cot = (wet_block * jnp.dot(couple.T, misfit, precision=PRECISE)).astype(jnp.bfloat16)
        second_cot = (
            jnp.einsum("ho,on->hn", w_out, flux_cot, preferred_element_type=jnp.float32)
            * silu_slope(pre_second)
        ).astype(jnp.bfloat16)
        first_cot = (
            jnp.einsum("hk,kn->hn", w_mid, second_cot, preferred_element_type=jnp.float32)
            * silu_slope(pre_first)
        ).astype(jnp.bfloat16)
        feature_cot = jnp.einsum("fh,hn->fn", w_in, first_cot, preferred_element_type=jnp.float32)
        additions = (
            jnp.einsum("fn,hn->fh", feature_block, first_cot, preferred_element_type=jnp.float32),
            jnp.sum(first_cot.astype(jnp.float32), axis=1),
            jnp.einsum("hn,kn->hk", hidden_first, second_cot, preferred_element_type=jnp.float32),
            jnp.sum(second_cot.astype(jnp.float32), axis=1),
            jnp.einsum("hn,on->ho", hidden_second, flux_cot, preferred_element_type=jnp.float32),
            jnp.sum(flux_cot.astype(jnp.float32), axis=1),
        )
        new_fields = lax.dynamic_update_slice_in_dim(new_fields, updated, offset, 1)
        misfits = lax.dynamic_update_slice_in_dim(misfits, misfit, offset, 1)
        feature_cots = lax.dynamic_update_slice_in_dim(feature_cots, feature_cot, offset, 1)
        return (new_fields, misfits, feature_cots, jax.tree.map(jnp.add, gradients, additions))

    initial = (
        jnp.zeros((channels, cell_count), jnp.float32),
        jnp.zeros((channels, cell_count), jnp.float32),
        jnp.zeros((2 * channels, cell_count), jnp.float32),
        (
            jnp.zeros(w_in.shape, jnp.float32),
            jnp.zeros(b_in.shape, jnp.float32),
            jnp.zeros(w_mid.shape, jnp.float32),
            jnp.zeros(b_mid.shape, jnp.float32),
            jnp.zeros(w_out.shape, jnp.float32),
            jnp.zeros(b_out.shape, jnp.float32),
        ),
    )
    new_fields, misfits, feature_cots, gradients = lax.fori_loop(
        0, cell_count // block_size, advance, initial
    )
    back_lap = laplace((diff_mask * misfits).reshape(channels, tile_rows, tile_width), on_fold)
    own_cot = jnp.where(is_ocean, feature_cots[channels:], feature_cots[:channels]).reshape(
        channels, tile_rows, tile_width
    )
    other_cot = jnp.where(is_ocean, feature_cots[:channels], feature_cots[channels:]).reshape(
        channels, tile_rows, tile_width
    )
    going_back = jnp.einsum("tk,ctj->kcj", landing, other_cot, precision=PRECISE).astype(
        jnp.bfloat16
    )
    returned = return_route(going_back.reshape(peer_count, slot_count, channels, tile_width))
    spread = (
        jnp.einsum(
            "kcj,kij->kci",
            returned.reshape(pair_count, channels, tile_width),
            kernels,
            preferred_element_type=jnp.float32,
        )
        * live_mask
    )
    anchor = (row_index == source.reshape(1, pair_count)).astype(jnp.float32)
    remap_back = jnp.einsum("tk,kci->cti", anchor, spread, precision=PRECISE)
    adjoint_field = (
        misfits.reshape(channels, tile_rows, tile_width)
        + diffuse_rate[:, None, None] * back_lap
        + own_cot
        + remap_back
    )
    grad_first, bias_first, grad_second, bias_second, grad_third, bias_third = gradients
    grad_first, bias_first, grad_second, bias_second, grad_third, bias_third = lax.psum(
        (grad_first, bias_first, grad_second, bias_second, grad_third, bias_third),
        ("comp", "gy", "gx"),
    )
    scale = 1.0 / (cell_count * lax.axis_size("gy") * lax.axis_size("gx"))
    return (
        new_fields.reshape(1, channels, tile_rows, tile_width),
        adjoint_field.reshape(1, channels, tile_rows, tile_width),
        grad_first * scale,
        bias_first * scale,
        grad_second * scale,
        bias_second * scale,
        grad_third * scale,
        bias_third * scale,
    )


def solution(mesh):
    placed = (
        P("comp", None, "gy", "gx"),
        P("comp", None, "gy", "gx"),
        P("comp", "gy", "gx"),
        P(),
        P(),
        P(),
        P(),
        P(),
        P(),
        P(),
        P(),
        P("comp", "gy", "gx", None, None, None, None),
        P("comp", "gy", "gx", None, None),
        P("comp", "gy", "gx", None, None),
        P("comp", "gy", "gx", None),
    )
    return jax.shard_map(
        shards,
        mesh=mesh,
        in_specs=placed,
        out_specs=(
            P("comp", None, "gy", "gx"),
            P("comp", None, "gy", "gx"),
            P(),
            P(),
            P(),
            P(),
            P(),
            P(),
        ),
        check_vma=False,
    )
```

profile of v0, /device:TPU:0, one launch (start us, length us, event | category | flops | bytes accessed | tf_op | source)
XLA Modules:
  0.0 382.0 jit_solution(18036116100139440150)
XLA Ops:
  10.0 3.1 collective-permute-start.4
  14.3 3.8 %collective-permute-start.2 = (f32[8,1,128]{1,2,0:T(8,128)}, f32[8,1,128]{1,2,0:T(8,128)}, u32[]{:S(2)}, u32[]{:S(2)}) collective-permute-start(f32[8,1,128]{1,2,0:T(8,128)} %get-tuple-element.628), channel_id=1, source_target_pairs={{0,4},{4,8},{8,12},{1,5},{5,9},{9,13},{2,6},{6,10},{10,14},{3,7},{... | collective-permute-start | bytes 12296 | tf_op jit(solution)/shard_map/ppermute | solution.py:18
  18.1 2.5 collective-permute-start
  25.0 6.2 %all-to-all-start = ((f32[16,4,8,128]{3,2,1,0:T(8,128)}), f32[16,4,8,128]{3,2,1,0:T(8,128)}, u32[]{:S(2)}, u32[]{:S(2)}) async-start(f32[16,4,8,128]{3,2,1,0:T(8,128)} %bitcast.7), calls=%async_computation | async-start | bytes 524288 | tf_op jit(solution)/shard_map/all_to_all | solution.py:61
  32.8 2.8 collective-permute-start.5
  37.8 3.1 collective-permute-done.5
  44.0 2.7 scatter-add.6
  51.9 2.6 copy_bitcast_fusion.4
  54.5 3.9 %collective-permute-done.6 = f32[16,4,8,128]{3,2,1,0:T(8,128)S(1)} collective-permute-done((f32[16,4,8,128]{3,2,1,0:T(8,128)}, f32[16,4,8,128]{3,2,1,0:T(8,128)S(1)}, u32[]{:S(2)}, u32[]{:S(2)}) %collective-permute-start.6) | collective-permute-done | bytes 262176 | tf_op jit(solution)/shard_map/ppermute | solution.py:34
  62.6 104.6 %while.32 = (s32[]{:T(128)}, f32[8,16384]{1,0:T(8,128)}, f32[8,16384]{1,0:T(8,128)}, f32[16,16384]{1,0:T(8,128)}, f32[16,256]{1,0:T(8,128)S(1)}, /*index=5*/f32[...) while((s32[]{:T(128)}, f32[8,16384]{1,0:T(8,128)}, ...), condition=%wide.region_4.5_spmd.clone, body=%wide.region_0.4_spmd.clone.sunk | while | flops 890530304 | bytes 47954832 | solution.py:199
  63.7 2.4 multiply_convert_fusion.7
  69.7 2.7 convert_reduce_fusion.7
  76.8 2.4 multiply_convert_fusion.7
  82.8 2.7 convert_reduce_fusion.7
  89.9 2.4 multiply_convert_fusion.7
  95.9 2.7 convert_reduce_fusion.7
  103.0 2.4 multiply_convert_fusion.7
  108.9 2.7 convert_reduce_fusion.7
  116.0 2.4 multiply_convert_fusion.7
  122.0 2.7 convert_reduce_fusion.7
  129.1 2.4 multiply_convert_fusion.7
  135.1 2.7 convert_reduce_fusion.7
  142.2 2.4 multiply_convert_fusion.7
  148.2 2.7 convert_reduce_fusion.7
  155.3 2.4 multiply_convert_fusion.7
  161.2 2.7 convert_reduce_fusion.7
  170.0 38.8 %all-reduce = (f32[16,256]{1,0:T(8,128)S(1)}, f32[256]{0:T(256)S(1)}, f32[256]{0:T(256)S(1)}, f32[256,4]{0,1:T(4,128)S(1)}, f32[4]{0:T(128)S(1)}) all-reduce(f32[16,256]{1,0:T(8,128)S(1)} %get-tuple-element.422, f32[256]{0:T(256)S(1)} %get-tuple-element.423, ...), channel_id=1, replica_groups=mesh['comp'=2,'gy'=4,'gx'=4] {'comp','gy','gx'}, use_global_device_ids=true, to_apply=%region_5.6 | all-reduce | flops 5636 | bytes 45088 | tf_op jit(solution)/shard_map/psum | solution.py:231
  214.9 3.8 %collective-permute-start.9 = (f32[8,1,128]{1,2,0:T(8,128)}, f32[8,1,128]{1,2,0:T(8,128)}, u32[]{:S(2)}, u32[]{:S(2)}) collective-permute-start(f32[8,1,128]{1,2,0:T(8,128)} %get-tuple-element.623), channel_id=1, source_target_pairs={{0,4},{4,8},{8,12},{1,5},{5,9},{9,13},{2,6},{6,10},{10,14},{3,7},{... | collective-permute-start | bytes 12296 | tf_op jit(solution)/shard_map/ppermute | solution.py:18
  224.2 7.0 %all-to-all-start.1 = ((bf16[16,4,8,128]{3,1,2,0:T(4,128)(2,1)}), bf16[16,4,8,128]{3,1,2,0:T(4,128)(2,1)S(1)}, u32[]{:S(2)}, u32[]{:S(2)}) async-start(bf16[16,4,8,128]{3,1,2,0:T(4,128)(2,1)} %copy.141), calls=%async_computation.1 | async-start | bytes 262144 | tf_op jit(solution)/shard_map/all_to_all | solution.py:67
  240.3 2.9 collective-permute-start.12
  250.8 116.6 %all-reduce.3.cloned.1.call-done = f32[256,256]{1,0:T(8,128)} async-done(((f32[256,256]{1,0:T(8,128)}), f32[256,256]{1,0:T(8,128)}) %all-reduce.3.cloned.1.call-update) | async-done | bytes 262160 | tf_op jit(solution)/shard_map/psum | solution.py:231
  370.4 2.7 fusion.18
  (360 shorter events, 123.2 us)
Async XLA Ops:
  7.2 16.4 %copy-start = (bf16[1,1,1,16,4,128,128]{6,5,4,3,2,1,0:T(8,128)(2,1)S(1)}, bf16[1,1,1,16,4,128,128]{6,5,4,3,2,1,0:T(8,128)(2,1)}, u32[]{:S(2)}) copy-start(bf16[1,1,1,16,4,128,128]{6,5,4,3,2,1,0:T(8,128)(2,1)} %param.32) | copy-start | bytes 6291460
  7.2 14.5 %copy-start.16 = (s32[1,1,1,16,4]{3,4,2,1,0:T(4,128)S(1)}, s32[1,1,1,16,4]{3,4,2,1,0:T(4,128)}, u32[]{:S(2)}) copy-start(s32[1,1,1,16,4]{3,4,2,1,0:T(4,128)} %param.33) | copy-start | bytes 772
  7.2 14.6 %copy-start.19 = (s32[1,1,1,16]{3,2,1,0:T(1,128)S(1)}, s32[1,1,1,16]{3,2,1,0:T(1,128)}, u32[]{:S(2)}) copy-start(s32[1,1,1,16]{3,2,1,0:T(1,128)} %param.35) | copy-start | bytes 196
  10.0 22.8 %collective-permute-start.4 = (f32[8,128]{1,0:T(8,128)S(1)}, f32[8,128]{1,0:T(8,128)S(1)}, u32[]{:S(2)}, u32[]{:S(2)}) collective-permute-start(f32[8,128]{1,0:T(8,128)S(1)} %rev.6), channel_id=1, source_target_pairs={{0,1},{1,0},{2,3},{3,2},{4,5},{5,4},{6,7},{7,6},{8,9},{9,8},{10,11... | collective-permute-start | bytes 12296 | tf_op jit(solution)/shard_map/ppermute | solution.py:34
  13.0 22.6 %collective-permute-start.3 = (f32[8,1,128]{1,2,0:T(8,128)}, f32[8,1,128]{1,2,0:T(8,128)}, u32[]{:S(2)}, u32[]{:S(2)}) collective-permute-start(f32[8,1,128]{1,2,0:T(8,128)} %get-tuple-element.630), channel_id=1, source_target_pairs={{4,0},{8,4},{12,8},{5,1},{9,5},{13,9},{6,2},{10,6},{14,10},{7,3},{... | collective-permute-start | bytes 12296 | tf_op jit(solution)/shard_map/ppermute | solution.py:20
  14.3 32.4 %collective-permute-start.2 = (f32[8,1,128]{1,2,0:T(8,128)}, f32[8,1,128]{1,2,0:T(8,128)}, u32[]{:S(2)}, u32[]{:S(2)}) collective-permute-start(f32[8,1,128]{1,2,0:T(8,128)} %get-tuple-element.628), channel_id=1, source_target_pairs={{0,4},{4,8},{8,12},{1,5},{5,9},{9,13},{2,6},{6,10},{10,14},{3,7},{... | collective-permute-start | bytes 12296 | tf_op jit(solution)/shard_map/ppermute | solution.py:18
  18.1 28.6 %collective-permute-start = (f32[8,128,1]{1,2,0:T(1,128)S(1)}, f32[8,128,1]{1,2,0:T(1,128)S(1)}, u32[]{:S(2)}, u32[]{:S(2)}) collective-permute-start(f32[8,128,1]{1,2,0:T(1,128)S(1)} %get-tuple-element.626), channel_id=1, source_target_pairs={{1,0},{2,1},{3,2},{0,3},{5,4},{6,5},{7,6},{4,7},{9,8},{10,9},{11,1... | collective-permute-start | bytes 12296 | tf_op jit(solution)/shard_map/ppermute | solution.py:20
  20.7 26.1 %collective-permute-start.1 = (f32[8,128,1]{1,2,0:T(1,128)S(1)}, f32[8,128,1]{1,2,0:T(1,128)S(1)}, u32[]{:S(2)}, u32[]{:S(2)}) collective-permute-start(f32[8,128,1]{1,2,0:T(1,128)S(1)} %get-tuple-element.627), channel_id=1, source_target_pairs={{0,1},{1,2},{2,3},{3,0},{4,5},{5,6},{6,7},{7,4},{8,9},{9,10},{10,1... | collective-permute-start | bytes 12296 | tf_op jit(solution)/shard_map/ppermute | solution.py:18
  20.7 10.5 %copy-start.18 = (f32[2,8,4]{1,2,0:T(4,128)S(1)}, f32[2,8,4]{1,2,0:T(4,128)}, u32[]{:S(2)}) copy-start(f32[2,8,4]{1,2,0:T(4,128)} %param.25) | copy-start | bytes 772
  20.7 10.5 %copy-start.22 = (f32[2,8]{1,0:T(2,128)S(1)}, f32[2,8]{1,0:T(2,128)}, u32[]{:S(2)}) copy-start(f32[2,8]{1,0:T(2,128)} %param.24) | copy-start | bytes 196
  20.7 10.5 %copy-start.12 = (s32[1,128,128]{2,1,0:T(8,128)S(1)}, s32[1,128,128]{2,1,0:T(8,128)}, u32[]{:S(2)}) copy-start(s32[1,128,128]{2,1,0:T(8,128)} %param.23) | copy-start | bytes 196612
  20.7 10.7 %copy-start.3 = (f32[1,8,128,128]{3,2,1,0:T(8,128)S(1)}, f32[1,8,128,128]{3,2,1,0:T(8,128)}, u32[]{:S(2)}) copy-start(f32[1,8,128,128]{3,2,1,0:T(8,128)} %param.21) | copy-start | bytes 1572868
  23.6 9.0 %copy-start.17 = (s32[1,1,1,16,4]{3,4,2,1,0:T(4,128)S(1)}, s32[1,1,1,16,4]{3,4,2,1,0:T(4,128)}, u32[]{:S(2)}) copy-start(s32[1,1,1,16,4]{3,4,2,1,0:T(4,128)} %param.34) | copy-start | bytes 772
  25.0 25.3 %all-to-all-start = ((f32[16,4,8,128]{3,2,1,0:T(8,128)}), f32[16,4,8,128]{3,2,1,0:T(8,128)}, u32[]{:S(2)}, u32[]{:S(2)}) async-start(f32[16,4,8,128]{3,2,1,0:T(8,128)} %bitcast.7), calls=%async_computation | async-start | bytes 524288 | tf_op jit(solution)/shard_map/all_to_all | solution.py:61
  32.8 8.1 %collective-permute-start.5 = (f32[8,128]{1,0:T(8,128)S(1)}, f32[8,128]{1,0:T(8,128)S(1)}, u32[]{:S(2)}, u32[]{:S(2)}) collective-permute-start(f32[8,128]{1,0:T(8,128)S(1)} %collective-permute-done.4), channel_id=1, source_target_pairs={{0,2},{2,0},{1,3},{3,1},{4,6},{6,4},{5,7},{7,5},{8,10},{10,8},{9,1... | collective-permute-start | bytes 12296 | tf_op jit(solution)/shard_map/ppermute | solution.py:34
  50.3 8.1 %collective-permute-start.6 = (f32[16,4,8,128]{3,2,1,0:T(8,128)}, f32[16,4,8,128]{3,2,1,0:T(8,128)S(1)}, u32[]{:S(2)}, u32[]{:S(2)}) collective-permute-start(f32[16,4,8,128]{3,2,1,0:T(8,128)} %all-to-all-done), channel_id=1, source_target_pairs={{0,16},{16,0},{1,17},{17,1},{2,18},{18,2},{3,19},{19,3},{4,20},{20... | collective-permute-start | bytes 786440 | tf_op jit(solution)/shard_map/ppermute | solution.py:34
  59.3 3.3 copy-start.9
  59.3 3.3 copy-start.13
  59.3 3.3 copy-start.14
  59.3 3.3 copy-start.15
  59.4 3.2 copy-start.23
  211.8 28.5 %collective-permute-start.11 = (f32[8,128]{1,0:T(8,128)S(1)}, f32[8,128]{1,0:T(8,128)S(1)}, u32[]{:S(2)}, u32[]{:S(2)}) collective-permute-start(f32[8,128]{1,0:T(8,128)S(1)} %rev.7), channel_id=1, source_target_pairs={{0,1},{1,0},{2,3},{3,2},{4,5},{5,4},{6,7},{7,6},{8,9},{9,8},{10,11... | collective-permute-start | bytes 12296 | tf_op jit(solution)/shard_map/ppermute | solution.py:34
  213.6 29.6 %collective-permute-start.10 = (f32[8,1,128]{1,2,0:T(8,128)}, f32[8,1,128]{1,2,0:T(8,128)}, u32[]{:S(2)}, u32[]{:S(2)}) collective-permute-start(f32[8,1,128]{1,2,0:T(8,128)} %get-tuple-element.625), channel_id=1, source_target_pairs={{4,0},{8,4},{12,8},{5,1},{9,5},{13,9},{6,2},{10,6},{14,10},{7,3},{... | collective-permute-start | bytes 12296 | tf_op jit(solution)/shard_map/ppermute | solution.py:20
  214.9 155.4 %collective-permute-start.9 = (f32[8,1,128]{1,2,0:T(8,128)}, f32[8,1,128]{1,2,0:T(8,128)}, u32[]{:S(2)}, u32[]{:S(2)}) collective-permute-start(f32[8,1,128]{1,2,0:T(8,128)} %get-tuple-element.623), channel_id=1, source_target_pairs={{0,4},{4,8},{8,12},{1,5},{5,9},{9,13},{2,6},{6,10},{10,14},{3,7},{... | collective-permute-start | bytes 12296 | tf_op jit(solution)/shard_map/ppermute | solution.py:18
  218.7 151.6 %collective-permute-start.7 = (f32[8,128,1]{1,2,0:T(1,128)S(1)}, f32[8,128,1]{1,2,0:T(1,128)S(1)}, u32[]{:S(2)}, u32[]{:S(2)}) collective-permute-start(f32[8,128,1]{1,2,0:T(1,128)S(1)} %get-tuple-element.621), channel_id=1, source_target_pairs={{1,0},{2,1},{3,2},{0,3},{5,4},{6,5},{7,6},{4,7},{9,8},{10,9},{11,1... | collective-permute-start | bytes 12296 | tf_op jit(solution)/shard_map/ppermute | solution.py:20
  221.0 149.4 %collective-permute-start.8 = (f32[8,128,1]{1,2,0:T(1,128)S(1)}, f32[8,128,1]{1,2,0:T(1,128)S(1)}, u32[]{:S(2)}, u32[]{:S(2)}) collective-permute-start(f32[8,128,1]{1,2,0:T(1,128)S(1)} %get-tuple-element.622), channel_id=1, source_target_pairs={{0,1},{1,2},{2,3},{3,0},{4,5},{5,6},{6,7},{7,4},{8,9},{9,10},{10,1... | collective-permute-start | bytes 12296 | tf_op jit(solution)/shard_map/ppermute | solution.py:18
  223.1 12.3 %copy-start.4 = (f32[8,16384]{1,0:T(8,128)S(1)}, f32[8,16384]{1,0:T(8,128)}, u32[]{:S(2)}) copy-start(f32[8,16384]{1,0:T(8,128)} %get-tuple-element.420) | copy-start | bytes 1572868
  224.2 26.0 %all-to-all-start.1 = ((bf16[16,4,8,128]{3,1,2,0:T(4,128)(2,1)}), bf16[16,4,8,128]{3,1,2,0:T(4,128)(2,1)S(1)}, u32[]{:S(2)}, u32[]{:S(2)}) async-start(bf16[16,4,8,128]{3,1,2,0:T(4,128)(2,1)} %copy.141), calls=%async_computation.1 | async-start | bytes 262144 | tf_op jit(solution)/shard_map/all_to_all | solution.py:67
  231.2 136.2 %all-reduce.3.cloned.1.call-start = ((), (), s32[]{:S(2)}) async-start(), calls=%async_computation.2 | async-start | bytes 524288 | tf_op jit(solution)/shard_map/psum | solution.py:231
  240.3 4.6 %collective-permute-start.12 = (f32[8,128]{1,0:T(8,128)S(1)}, f32[8,128]{1,0:T(8,128)S(1)}, u32[]{:S(2)}, u32[]{:S(2)}) collective-permute-start(f32[8,128]{1,0:T(8,128)S(1)} %collective-permute-done.11), channel_id=1, source_target_pairs={{0,2},{2,0},{1,3},{3,1},{4,6},{6,4},{5,7},{7,5},{8,10},{10,8},{9,1... | collective-permute-start | bytes 12296 | tf_op jit(solution)/shard_map/ppermute | solution.py:34
  250.2 118.9 %collective-permute-start.13 = (bf16[16,4,8,128]{3,1,2,0:T(4,128)(2,1)S(1)}, bf16[16,4,8,128]{3,1,2,0:T(4,128)(2,1)S(1)}, u32[]{:S(2)}, u32[]{:S(2)}) collective-permute-start(bf16[16,4,8,128]{3,1,2,0:T(4,128)(2,1)S(1)} %all-to-all-done.1), channel_id=1, source_target_pairs={{0,16},{16,0},{1,17},{17,1},{2,18},{18,2},{3,19},{19,3},{4,20},{20... | collective-permute-start | bytes 393224 | tf_op jit(solution)/shard_map/ppermute | solution.py:34
  367.4 3.0 copy-start.8
  (65 other events, 116.1 us)
Sparse Core Ops, SparseCore 0:
  240.4 126.9 all-reduce.2
where the time goes:
time: 384 us; the launch traced here: 382 us
  waiting for transfers between devices  124 us (32%)
  matrix products  105 us (27%)
  starting transfers between devices  41.2 us (11%)
  local copies, waits for them, and re-layouts  38.9 us (10%)
  blocking collectives  38.8 us (10%)
  other arithmetic  18.7 us (5%)
  between operations  14.5 us (4%)
    psum x1, waiting for transfers between devices, shards(): lax.psum((grad_first, bias_first, grad_second, bias_second, grad_third, b...  117 us
    psum x1, blocking collectives, shards(): lax.psum((grad_first, bias_first, grad_second, bias_second, grad_third, b...  38.8 us
    dot_general x8, matrix products, advance(): jnp.einsum('ho,on->hn', w_out, flux_cot, preferred_element_type=jnp.float32)  21.6 us
    dot_general x8, matrix products, advance(): jnp.einsum('hk,hn->kn', w_mid, hidden_first, preferred_element_type=jnp.f...  18.9 us
    dot_general x8, matrix products, advance(): jnp.dot(couple, fluxes, precision=PRECISE)  14.6 us
    ppermute x6, starting transfers between devices, partner(): return lax.ppermute(block, axis, route)  12.7 us
    unnamed x41, local copies, waits for them, and re-layouts  9.63 us
    dot_general x8, matrix products, advance(): jnp.dot(couple.T, misfit, precision=PRECISE)  9.23 us
  transfers between devices with their start and end apart: 17, of which 4 were waited for; matrix products, arithmetic and copies ran while one was open for 11% of the time, Pallas kernels for 0%

commit v1 on v0

--- a/solution.py
+++ b/solution.py
@@ -86,6 +86,12 @@
     remap_target,
     remap_count,
 ):
+
+    def heads_derive(m):
+        for dev_i in ("comp", ("gy", "gx")):
+            m = lax.psum(m, dev_i)
+        return m
+
     comp_index = lax.axis_index("comp")
     is_ocean = comp_index == 1
     on_fold = jnp.logical_and(is_ocean, lax.axis_index("gy") == lax.axis_size("gy") - 1)
@@ -228,9 +234,8 @@
         + remap_back
     )
     grad_first, bias_first, grad_second, bias_second, grad_third, bias_third = gradients
-    grad_first, bias_first, grad_second, bias_second, grad_third, bias_third = lax.psum(
-        (grad_first, bias_first, grad_second, bias_second, grad_third, bias_third),
-        ("comp", "gy", "gx"),
+    grad_first, bias_first, grad_second, bias_second, grad_third, bias_third = heads_derive(
+        (grad_first, bias_first, grad_second, bias_second, grad_third, bias_third)
     )
     scale = 1.0 / (cell_count * lax.axis_size("gy") * lax.axis_size("gx"))
     return (

time: 384 us -> 392 us (1.021)
  blocking collectives: 38.8 us -> 66.2 us
  waiting for transfers between devices: 124 us -> 109 us
  starting transfers between devices: 41.2 us -> 36.7 us
    psum x1 -> x2, blocking collectives: 38.8 us -> 66.2 us  [heads_derive(): m = lax.psum(m, dev_i)]
    psum x1 -> x2, waiting for transfers between devices: 117 us -> 100 us  [heads_derive(): m = lax.psum(m, dev_i)]
  transfers between devices with their start and end apart: 17 -> 18, of which waited for: 4 -> 5; matrix products, arithmetic and copies ran while one was open for 11% -> 12% of each run, Pallas kernels for 0% -> 0%
where the time goes in v1:
time: 392 us; the launch traced here: 390 us
  waiting for transfers between devices  109 us (28%)
  matrix products  105 us (27%)
  blocking collectives  66.2 us (17%)
  local copies, waits for them, and re-layouts  38.8 us (10%)
  starting transfers between devices  36.7 us (9%)
  other arithmetic  18.6 us (5%)
  between operations  14.6 us (4%)
    psum x2, waiting for transfers between devices, heads_derive(): m = lax.psum(m, dev_i)  100 us
    psum x2, blocking collectives, heads_derive(): m = lax.psum(m, dev_i)  66.2 us
    dot_general x8, matrix products, advance(): jnp.einsum('ho,on->hn', w_out, flux_cot, preferred_element_type=jnp.float32)  21.6 us
    dot_general x8, matrix products, advance(): jnp.einsum('hk,hn->kn', w_mid, hidden_first, preferred_element_type=jnp.f...  19 us
    dot_general x8, matrix products, advance(): jnp.dot(couple, fluxes, precision=PRECISE)  14.6 us
    unnamed x41, local copies, waits for them, and re-layouts  9.63 us
    ppermute x6, starting transfers between devices, partner(): return lax.ppermute(block, axis, route)  9.58 us
    dot_general x8, matrix products, advance(): jnp.dot(couple.T, misfit, precision=PRECISE)  9.23 us
  transfers between devices with their start and end apart: 18, of which 5 were waited for; matrix products, arithmetic and copies ran while one was open for 12% of the time, Pallas kernels for 0%

profile of v1, /device:TPU:0, one launch (start us, length us, event | category | flops | bytes accessed | tf_op | source)
XLA Modules:
  0.0 389.6 jit_solution(11951899733540797867)
XLA Ops:
  10.0 3.1 collective-permute-start.4
  14.3 3.8 collective-permute-start.2
  18.1 2.5 collective-permute-start
  25.0 6.2 %all-to-all-start = ((f32[16,4,8,128]{3,2,1,0:T(8,128)}), f32[16,4,8,128]{3,2,1,0:T(8,128)}, u32[]{:S(2)}, u32[]{:S(2)}) async-start(f32[16,4,8,128]{3,2,1,0:T(8,128)} %bitcast.7), calls=%async_computation | async-start | bytes 524288 | tf_op jit(solution)/shard_map/all_to_all | solution.py:61
  32.8 2.8 collective-permute-start.5
  37.8 3.1 collective-permute-done.5
  44.0 2.7 scatter-add.6
  51.8 2.6 copy_bitcast_fusion.4
  54.5 3.9 %collective-permute-done.6 = f32[16,4,8,128]{3,2,1,0:T(8,128)S(1)} collective-permute-done((f32[16,4,8,128]{3,2,1,0:T(8,128)}, f32[16,4,8,128]{3,2,1,0:T(8,128)S(1)}, u32[]{:S(2)}, u32[]{:S(2)}) %collective-permute-start.6) | collective-permute-done | bytes 262176 | tf_op jit(solution)/shard_map/ppermute | solution.py:34
  62.6 104.7 %while.32 = (s32[]{:T(128)}, f32[8,16384]{1,0:T(8,128)}, f32[8,16384]{1,0:T(8,128)}, f32[16,16384]{1,0:T(8,128)}, f32[16,256]{1,0:T(8,128)S(1)}, /*index=5*/f32[...) while((s32[]{:T(128)}, f32[8,16384]{1,0:T(8,128)}, ...), condition=%wide.region_4.5_spmd.clone, body=%wide.region_0.4_spmd.clone.sunk | while | flops 890530304 | bytes 47954832 | solution.py:205
  63.7 2.4 multiply_convert_fusion.7
  69.7 2.7 convert_reduce_fusion.7
  76.8 2.4 multiply_convert_fusion.7
  82.8 2.7 convert_reduce_fusion.7
  89.9 2.4 multiply_convert_fusion.7
  95.9 2.7 convert_reduce_fusion.7
  103.0 2.4 multiply_convert_fusion.7
  109.0 2.7 convert_reduce_fusion.7
  116.1 2.4 multiply_convert_fusion.7
  122.1 2.7 convert_reduce_fusion.7
  129.2 2.4 multiply_convert_fusion.7
  135.2 2.7 convert_reduce_fusion.7
  148.2 2.7 convert_reduce_fusion.7
  161.3 2.7 convert_reduce_fusion.7
  170.0 8.3 %all-reduce.1 = (f32[16,256]{1,0:T(8,128)S(1)}, f32[256]{0:T(256)S(1)}, f32[256]{0:T(256)S(1)}, f32[256,4]{0,1:T(4,128)S(1)}, f32[4]{0:T(128)S(1)}) all-reduce(f32[16,256]{1,0:T(8,128)S(1)} %get-tuple-element.422, f32[256]{0:T(256)S(1)} %get-tuple-element.423, ...), channel_id=1, replica_groups=mesh['comp'=2,'gy'=4,'gx'=4] {'comp'}, use_global_device_ids=true, to_apply=%region_5.6 | all-reduce | flops 5636 | bytes 45088 | tf_op jit(solution)/shard_map/psum | solution.py:92
  178.3 57.9 %all-reduce = (f32[16,256]{1,0:T(8,128)S(1)}, f32[256]{0:T(256)S(1)}, f32[256]{0:T(256)S(1)}, f32[256,4]{0,1:T(4,128)S(1)}, f32[4]{0:T(128)S(1)}) all-reduce(f32[16,256]{1,0:T(8,128)S(1)} %get-tuple-element.604, f32[256]{0:T(256)S(1)} %get-tuple-element.605, ...), channel_id=1, replica_groups=mesh['comp'=2,'gy'=4,'gx'=4] {'gy','gx'}, use_global_device_ids=true, to_apply=%region_6.7 | all-reduce | flops 5636 | bytes 45088 | tf_op jit(solution)/shard_map/psum | solution.py:92
  243.5 5.4 %all-to-all-start.1 = ((bf16[16,4,8,128]{3,1,2,0:T(4,128)(2,1)}), bf16[16,4,8,128]{3,1,2,0:T(4,128)(2,1)S(1)}, u32[]{:S(2)}, u32[]{:S(2)}) async-start(bf16[16,4,8,128]{3,1,2,0:T(4,128)(2,1)} %copy.141), calls=%async_computation.1 | async-start | bytes 262144 | tf_op jit(solution)/shard_map/all_to_all | solution.py:67
  249.4 3.1 collective-permute-start.9
  252.5 3.4 collective-permute-start.7
  274.8 13.2 %all-reduce.5.cloned.1.call-done = f32[256,256]{1,0:T(8,128)} async-done(((f32[256,256]{1,0:T(8,128)}), f32[256,256]{1,0:T(8,128)}) %all-reduce.5.cloned.1.call-update) | async-done | bytes 262160 | tf_op jit(solution)/shard_map/psum | solution.py:92
  289.3 2.7 fusion.18
  294.1 87.1 %all-reduce.7.cloned.1.call-done = f32[256,256]{1,0:T(8,128)} async-done(((f32[256,256]{1,0:T(8,128)}), f32[256,256]{1,0:T(8,128)}) %all-reduce.7.cloned.1.call-update) | async-done | bytes 262160 | tf_op jit(solution)/shard_map/psum | solution.py:92
  (364 shorter events, 126.2 us)
Async XLA Ops:
  7.2 16.4 %copy-start = (bf16[1,1,1,16,4,128,128]{6,5,4,3,2,1,0:T(8,128)(2,1)S(1)}, bf16[1,1,1,16,4,128,128]{6,5,4,3,2,1,0:T(8,128)(2,1)}, u32[]{:S(2)}) copy-start(bf16[1,1,1,16,4,128,128]{6,5,4,3,2,1,0:T(8,128)(2,1)} %param.32) | copy-start | bytes 6291460
  7.2 14.5 %copy-start.16 = (s32[1,1,1,16,4]{3,4,2,1,0:T(4,128)S(1)}, s32[1,1,1,16,4]{3,4,2,1,0:T(4,128)}, u32[]{:S(2)}) copy-start(s32[1,1,1,16,4]{3,4,2,1,0:T(4,128)} %param.33) | copy-start | bytes 772
  7.2 14.7 %copy-start.19 = (s32[1,1,1,16]{3,2,1,0:T(1,128)S(1)}, s32[1,1,1,16]{3,2,1,0:T(1,128)}, u32[]{:S(2)}) copy-start(s32[1,1,1,16]{3,2,1,0:T(1,128)} %param.35) | copy-start | bytes 196
  10.0 22.8 %collective-permute-start.4 = (f32[8,128]{1,0:T(8,128)S(1)}, f32[8,128]{1,0:T(8,128)S(1)}, u32[]{:S(2)}, u32[]{:S(2)}) collective-permute-start(f32[8,128]{1,0:T(8,128)S(1)} %rev.6), channel_id=1, source_target_pairs={{0,1},{1,0},{2,3},{3,2},{4,5},{5,4},{6,7},{7,6},{8,9},{9,8},{10,11... | collective-permute-start | bytes 12296 | tf_op jit(solution)/shard_map/ppermute | solution.py:34
  13.0 22.6 %collective-permute-start.3 = (f32[8,1,128]{1,2,0:T(8,128)}, f32[8,1,128]{1,2,0:T(8,128)}, u32[]{:S(2)}, u32[]{:S(2)}) collective-permute-start(f32[8,1,128]{1,2,0:T(8,128)} %get-tuple-element.635), channel_id=1, source_target_pairs={{4,0},{8,4},{12,8},{5,1},{9,5},{13,9},{6,2},{10,6},{14,10},{7,3},{... | collective-permute-start | bytes 12296 | tf_op jit(solution)/shard_map/ppermute | solution.py:20
  14.3 32.4 %collective-permute-start.2 = (f32[8,1,128]{1,2,0:T(8,128)}, f32[8,1,128]{1,2,0:T(8,128)}, u32[]{:S(2)}, u32[]{:S(2)}) collective-permute-start(f32[8,1,128]{1,2,0:T(8,128)} %get-tuple-element.633), channel_id=1, source_target_pairs={{0,4},{4,8},{8,12},{1,5},{5,9},{9,13},{2,6},{6,10},{10,14},{3,7},{... | collective-permute-start | bytes 12296 | tf_op jit(solution)/shard_map/ppermute | solution.py:18
  18.1 28.5 %collective-permute-start = (f32[8,128,1]{1,2,0:T(1,128)S(1)}, f32[8,128,1]{1,2,0:T(1,128)S(1)}, u32[]{:S(2)}, u32[]{:S(2)}) collective-permute-start(f32[8,128,1]{1,2,0:T(1,128)S(1)} %get-tuple-element.631), channel_id=1, source_target_pairs={{1,0},{2,1},{3,2},{0,3},{5,4},{6,5},{7,6},{4,7},{9,8},{10,9},{11,1... | collective-permute-start | bytes 12296 | tf_op jit(solution)/shard_map/ppermute | solution.py:20
  20.7 26.0 %collective-permute-start.1 = (f32[8,128,1]{1,2,0:T(1,128)S(1)}, f32[8,128,1]{1,2,0:T(1,128)S(1)}, u32[]{:S(2)}, u32[]{:S(2)}) collective-permute-start(f32[8,128,1]{1,2,0:T(1,128)S(1)} %get-tuple-element.632), channel_id=1, source_target_pairs={{0,1},{1,2},{2,3},{3,0},{4,5},{5,6},{6,7},{7,4},{8,9},{9,10},{10,1... | collective-permute-start | bytes 12296 | tf_op jit(solution)/shard_map/ppermute | solution.py:18
  20.7 10.5 %copy-start.18 = (f32[2,8,4]{1,2,0:T(4,128)S(1)}, f32[2,8,4]{1,2,0:T(4,128)}, u32[]{:S(2)}) copy-start(f32[2,8,4]{1,2,0:T(4,128)} %param.25) | copy-start | bytes 772
  20.7 10.5 %copy-start.22 = (f32[2,8]{1,0:T(2,128)S(1)}, f32[2,8]{1,0:T(2,128)}, u32[]{:S(2)}) copy-start(f32[2,8]{1,0:T(2,128)} %param.24) | copy-start | bytes 196
  20.7 10.5 %copy-start.12 = (s32[1,128,128]{2,1,0:T(8,128)S(1)}, s32[1,128,128]{2,1,0:T(8,128)}, u32[]{:S(2)}) copy-start(s32[1,128,128]{2,1,0:T(8,128)} %param.23) | copy-start | bytes 196612
  20.7 10.6 %copy-start.3 = (f32[1,8,128,128]{3,2,1,0:T(8,128)S(1)}, f32[1,8,128,128]{3,2,1,0:T(8,128)}, u32[]{:S(2)}) copy-start(f32[1,8,128,128]{3,2,1,0:T(8,128)} %param.21) | copy-start | bytes 1572868
  23.6 9.0 %copy-start.17 = (s32[1,1,1,16,4]{3,4,2,1,0:T(4,128)S(1)}, s32[1,1,1,16,4]{3,4,2,1,0:T(4,128)}, u32[]{:S(2)}) copy-start(s32[1,1,1,16,4]{3,4,2,1,0:T(4,128)} %param.34) | copy-start | bytes 772
  25.0 25.3 %all-to-all-start = ((f32[16,4,8,128]{3,2,1,0:T(8,128)}), f32[16,4,8,128]{3,2,1,0:T(8,128)}, u32[]{:S(2)}, u32[]{:S(2)}) async-start(f32[16,4,8,128]{3,2,1,0:T(8,128)} %bitcast.7), calls=%async_computation | async-start | bytes 524288 | tf_op jit(solution)/shard_map/all_to_all | solution.py:61
  32.8 8.2 %collective-permute-start.5 = (f32[8,128]{1,0:T(8,128)S(1)}, f32[8,128]{1,0:T(8,128)S(1)}, u32[]{:S(2)}, u32[]{:S(2)}) collective-permute-start(f32[8,128]{1,0:T(8,128)S(1)} %collective-permute-done.4), channel_id=1, source_target_pairs={{0,2},{2,0},{1,3},{3,1},{4,6},{6,4},{5,7},{7,5},{8,10},{10,8},{9,1... | collective-permute-start | bytes 12296 | tf_op jit(solution)/shard_map/ppermute | solution.py:34
  50.3 8.1 %collective-permute-start.6 = (f32[16,4,8,128]{3,2,1,0:T(8,128)}, f32[16,4,8,128]{3,2,1,0:T(8,128)S(1)}, u32[]{:S(2)}, u32[]{:S(2)}) collective-permute-start(f32[16,4,8,128]{3,2,1,0:T(8,128)} %all-to-all-done), channel_id=1, source_target_pairs={{0,16},{16,0},{1,17},{17,1},{2,18},{18,2},{3,19},{19,3},{4,20},{20... | collective-permute-start | bytes 786440 | tf_op jit(solution)/shard_map/ppermute | solution.py:34
  59.3 3.3 copy-start.9
  59.3 3.3 copy-start.13
  59.3 3.3 copy-start.14
  59.3 3.3 copy-start.15
  59.3 3.3 copy-start.23
  238.7 26.2 %collective-permute-start.11 = (f32[8,128]{1,0:T(8,128)S(1)}, f32[8,128]{1,0:T(8,128)S(1)}, u32[]{:S(2)}, u32[]{:S(2)}) collective-permute-start(f32[8,128]{1,0:T(8,128)S(1)} %rev.7), channel_id=1, source_target_pairs={{0,1},{1,0},{2,3},{3,2},{4,5},{5,4},{6,7},{7,6},{8,9},{9,8},{10,11... | collective-permute-start | bytes 12296 | tf_op jit(solution)/shard_map/ppermute | solution.py:34
  239.0 27.1 %collective-permute-start.10 = (f32[8,1,128]{1,2,0:T(8,128)}, f32[8,1,128]{1,2,0:T(8,128)}, u32[]{:S(2)}, u32[]{:S(2)}) collective-permute-start(f32[8,1,128]{1,2,0:T(8,128)} %get-tuple-element.630), channel_id=1, source_target_pairs={{4,0},{8,4},{12,8},{5,1},{9,5},{13,9},{6,2},{10,6},{14,10},{7,3},{... | collective-permute-start | bytes 12296 | tf_op jit(solution)/shard_map/ppermute | solution.py:20
  242.4 17.6 %copy-start.4 = (f32[8,16384]{1,0:T(8,128)S(1)}, f32[8,16384]{1,0:T(8,128)}, u32[]{:S(2)}) copy-start(f32[8,16384]{1,0:T(8,128)} %get-tuple-element.420) | copy-start | bytes 1572868
  243.5 24.0 %all-to-all-start.1 = ((bf16[16,4,8,128]{3,1,2,0:T(4,128)(2,1)}), bf16[16,4,8,128]{3,1,2,0:T(4,128)(2,1)S(1)}, u32[]{:S(2)}, u32[]{:S(2)}) async-start(bf16[16,4,8,128]{3,1,2,0:T(4,128)(2,1)} %copy.141), calls=%async_computation.1 | async-start | bytes 262144 | tf_op jit(solution)/shard_map/all_to_all | solution.py:67
  248.8 39.2 %all-reduce.5.cloned.1.call-start = ((), (), s32[]{:S(2)}) async-start(), calls=%async_computation.2 | async-start | bytes 524288 | tf_op jit(solution)/shard_map/psum | solution.py:92
  249.4 39.9 %collective-permute-start.9 = (f32[8,1,128]{1,2,0:T(8,128)}, f32[8,1,128]{1,2,0:T(8,128)}, u32[]{:S(2)}, u32[]{:S(2)}) collective-permute-start(f32[8,1,128]{1,2,0:T(8,128)} %get-tuple-element.628), channel_id=1, source_target_pairs={{0,4},{4,8},{8,12},{1,5},{5,9},{9,13},{2,6},{6,10},{10,14},{3,7},{... | collective-permute-start | bytes 12296 | tf_op jit(solution)/shard_map/ppermute | solution.py:18
  252.5 36.8 %collective-permute-start.7 = (f32[8,128,1]{1,2,0:T(1,128)S(1)}, f32[8,128,1]{1,2,0:T(1,128)S(1)}, u32[]{:S(2)}, u32[]{:S(2)}) collective-permute-start(f32[8,128,1]{1,2,0:T(1,128)S(1)} %get-tuple-element.626), channel_id=1, source_target_pairs={{1,0},{2,1},{3,2},{0,3},{5,4},{6,5},{7,6},{4,7},{9,8},{10,9},{11,1... | collective-permute-start | bytes 12296 | tf_op jit(solution)/shard_map/ppermute | solution.py:20
  256.0 33.4 %collective-permute-start.8 = (f32[8,128,1]{1,2,0:T(1,128)S(1)}, f32[8,128,1]{1,2,0:T(1,128)S(1)}, u32[]{:S(2)}, u32[]{:S(2)}) collective-permute-start(f32[8,128,1]{1,2,0:T(1,128)S(1)} %get-tuple-element.627), channel_id=1, source_target_pairs={{0,1},{1,2},{2,3},{3,0},{4,5},{5,6},{6,7},{7,4},{8,9},{9,10},{10,1... | collective-permute-start | bytes 12296 | tf_op jit(solution)/shard_map/ppermute | solution.py:18
  264.8 116.3 %all-reduce.7.cloned.1.call-start = ((), (), s32[]{:S(2)}) async-start(), calls=%async_computation.3 | async-start | bytes 524288 | tf_op jit(solution)/shard_map/psum | solution.py:92
  264.9 4.6 %collective-permute-start.12 = (f32[8,128]{1,0:T(8,128)S(1)}, f32[8,128]{1,0:T(8,128)S(1)}, u32[]{:S(2)}, u32[]{:S(2)}) collective-permute-start(f32[8,128]{1,0:T(8,128)S(1)} %collective-permute-done.11), channel_id=1, source_target_pairs={{0,2},{2,0},{1,3},{3,1},{4,6},{6,4},{5,7},{7,5},{8,10},{10,8},{9,1... | collective-permute-start | bytes 12296 | tf_op jit(solution)/shard_map/ppermute | solution.py:34
  267.5 20.6 %collective-permute-start.13 = (bf16[16,4,8,128]{3,1,2,0:T(4,128)(2,1)S(1)}, bf16[16,4,8,128]{3,1,2,0:T(4,128)(2,1)S(1)}, u32[]{:S(2)}, u32[]{:S(2)}) collective-permute-start(bf16[16,4,8,128]{3,1,2,0:T(4,128)(2,1)S(1)} %all-to-all-done.1), channel_id=1, source_target_pairs={{0,16},{16,0},{1,17},{17,1},{2,18},{18,2},{3,19},{19,3},{4,20},{20... | collective-permute-start | bytes 393224 | tf_op jit(solution)/shard_map/ppermute | solution.py:34
  (66 other events, 115.8 us)
Sparse Core Ops, SparseCore 0:
  265.0 23.0 all-reduce.4
  291.4 89.6 all-reduce.6
